TPU v7x, 512 devices: a whole 4x8x8 slice. The times are simulated.
512 devices in a mesh: segment: 4 (over x), chan: 16 (over y, core), dp: 8 (over z).
Axes of the slice: x: 4, y: 8, z: 8, core: 2. Of those that a mesh axis runs over, the one named last changes fastest.
Arguments:
- grad_top: bfloat16 [8, 1536, 256], P('dp', None, 'chan'), may hold values from -6 to 6
- inputs_one: bfloat16 [4, 8, 1536, 256], P('segment', 'dp', 'chan'), may hold values from -6 to 6
- conv_one: bfloat16 [4, 8, 1536, 256], P('segment', 'dp', 'chan'), may hold values from -130 to 130
- inputs_two: bfloat16 [4, 8, 1536, 256], P('segment', 'dp', 'chan'), may hold values from -6 to 6
- conv_two: bfloat16 [4, 8, 1536, 256], P('segment', 'dp', 'chan'), may hold values from -130 to 130
- proj_weight: bfloat16 [4, 2, 1536, 1536], P('segment', None, 'chan'), may hold values from -0.15625 to 0.15625
- conv_weight: bfloat16 [4, 2, 1536, 432], P('segment', None, 'chan'), may hold values from -0.3125 to 0.3125
- norm_gain: float32 [4, 2, 1536], P('segment', None, 'chan'), may hold values from 0.1 to 1.9
- norm_bias: float32 [4, 2, 1536], P('segment', None, 'chan'), may hold values from -4 to 4
Outputs:
- grad_latent: bfloat16 [4, 8, 1536, 256], P('segment', 'dp', None, 'chan')
- grad_proj: float32 [4, 2, 1536, 1536], P('segment', None, 'chan')
- grad_conv: float32 [4, 2, 1536, 432], P('segment', None, 'chan')
- grad_gain: float32 [4, 2, 1536], P('segment', None, 'chan')
- grad_bias: float32 [4, 2, 1536], P('segment', None, 'chan')
All inputs are finite; a program needn't handle non-finite values.
Results may differ from a plain program's by a relative error of at most 0.009.
Values may be sent and summed in bfloat16 or wider, within the bound.
No kernel may reach another device: no remote copies, remote signals or barrier semaphores. Data moves between devices by JAX's collectives and lax.ppermute only.
A program may use at most 64 MiB of HBM per device.

v0:
```python
import jax
import jax.numpy as jnp
from jax import lax
from jax.sharding import PartitionSpec as P

GS = 48
WW = 64
NORM_EPS = 1e-05


def passed_along(block, axis, distance):
    devices = range(lax.axis_size(axis))
    route = [(i - distance, i) for i in devices if i - distance in devices]
    return lax.ppermute(block, axis, route)


def shifted_cells(values, step_row, step_col, img_width):
    length = values.shape[2]
    margin = img_width + 1
    padded = jnp.pad(values, ((0, 0), (0, 0), (margin, margin)))
    start_at = margin + step_row * img_width + step_col
    part_view = lax.slice_in_dim(padded, start_at, start_at + length, axis=2)
    column = jnp.arange(length, dtype=jnp.int32) % img_width
    inside = (column + step_col >= 0) & (column + step_col < img_width)
    return jnp.where(inside, part_view, jnp.zeros((), values.dtype))


def norm_forward(saved_pre, gain_vec, bias_vec):
    chans, positions = saved_pre.shape
    groups_here = chans // GS
    pre = saved_pre.astype(jnp.float32).reshape(groups_here, GS, positions)
    centre = jnp.mean(pre, axis=(1, 2), keepdims=True)
    varied = jnp.mean(jnp.square(pre - centre), axis=(1, 2), keepdims=True)
    inv_std = lax.rsqrt(varied + NORM_EPS)
    normed = (pre - centre) * inv_std
    gain_grid = gain_vec.reshape(groups_here, GS, 1)
    scaled = normed * gain_grid + bias_vec.reshape(groups_here, GS, 1)
    gate_vals = jax.nn.sigmoid(scaled)
    act_bf = (scaled * gate_vals).astype(jnp.bfloat16).reshape(chans, positions)
    return (normed, scaled, gate_vals, inv_std, gain_grid, act_bf)


def conv_backward(grad_act, norm_state, saved_in, w_conv):
    normed, scaled, gate_vals, inv_std, gain_grid, act_bf = norm_state
    groups_here, _, positions = normed.shape
    chans = groups_here * GS
    grad_act = grad_act.reshape(groups_here, GS, positions)
    grad_norm = grad_act * (gate_vals * (1.0 + scaled * (1.0 - gate_vals)))
    gain_grad = jnp.sum(grad_norm * normed, axis=2).reshape(chans)
    bias_grad = jnp.sum(grad_norm, axis=2).reshape(chans)
    weighted = grad_norm * gain_grid
    first_mean = jnp.mean(weighted, axis=(1, 2), keepdims=True)
    second_mean = jnp.mean(weighted * normed, axis=(1, 2), keepdims=True)
    grad_pre = (inv_std * (weighted - first_mean - normed * second_mean)).astype(jnp.bfloat16)
    saved_grid = saved_in.reshape(groups_here, GS, positions)
    taps_w = w_conv.reshape(groups_here, GS, 9, GS)
    conv_parts = []
    back_sum = jnp.zeros((groups_here, GS, positions), jnp.float32)
    for tap_row in (-1, 0, 1):
        for tap_col in (-1, 0, 1):
            tap_at = 3 * (tap_row + 1) + tap_col + 1
            source = shifted_cells(saved_grid, tap_row, tap_col, WW)
            conv_parts.append(
                jnp.einsum("gop,gjp->goj", grad_pre, source, preferred_element_type=jnp.float32)
            )
            spread_back = jnp.einsum(
                "goj,gop->gjp",
                taps_w[:, :, tap_at, :],
                grad_pre,
                preferred_element_type=jnp.float32,
            )
            back_sum = back_sum + shifted_cells(spread_back, -tap_row, -tap_col, WW)
    conv_grad = jnp.stack(conv_parts, axis=2).reshape(chans, 9 * GS)
    branch = back_sum.reshape(chans, positions).astype(jnp.bfloat16)
    return (branch, conv_grad, gain_grad, bias_grad)


def block_sharded(grad_slab, saved_in, saved_pre, w_proj, w_conv, gain_vec, bias_vec):
    norm_state = norm_forward(saved_pre, gain_vec, bias_vec)
    act_bf = norm_state[5]
    grad_piece = lax.all_gather(grad_slab, "chan", axis=1, tiled=True)
    fresh = jnp.dot(w_proj, grad_piece, preferred_element_type=jnp.float32)
    weight_acc = lax.dot_general(
        act_bf, grad_piece, (((1,), (1,)), ((), ())), preferred_element_type=jnp.float32
    )
    branch, conv_grad, gain_grad, bias_grad = conv_backward(fresh, norm_state, saved_in, w_conv)
    returned = lax.all_to_all(branch, "chan", split_axis=1, concat_axis=0, tiled=True)
    out_slab = (grad_slab.astype(jnp.float32) + returned.astype(jnp.float32)).astype(jnp.bfloat16)
    return (out_slab, (weight_acc, conv_grad, gain_grad, bias_grad))


def take_micro(saved_all, index_at):
    return lax.dynamic_index_in_dim(saved_all[0], index_at, 0, keepdims=False)


def per_device(
    grad_top,
    inputs_one,
    conv_one,
    inputs_two,
    conv_two,
    proj_weight,
    conv_weight,
    norm_gain,
    norm_bias,
):
    segments = lax.axis_size("segment")
    segment_at = lax.axis_index("segment")
    local_mb = grad_top.shape[0]
    chans = conv_one.shape[2]
    width_all = proj_weight.shape[3]
    ticks = local_mb + segments - 1
    initial = (
        jnp.zeros(grad_top.shape[1:], jnp.bfloat16),
        jnp.zeros((1,) + grad_top.shape, jnp.bfloat16),
        jnp.zeros((2, chans, width_all), jnp.float32),
        jnp.zeros((2, chans, 9 * GS), jnp.float32),
        jnp.zeros((2, chans), jnp.float32),
        jnp.zeros((2, chans), jnp.float32),
    )

    def one_tick(tick_at, running):
        received, latent, proj_acc, conv_acc, gain_acc, bias_acc = running
        micro_at = tick_at - (segments - 1 - segment_at)
        is_valid = (micro_at >= 0) & (micro_at < local_mb)
        safe_mb = jnp.clip(micro_at, 0, local_mb - 1)
        top_grad = lax.dynamic_index_in_dim(grad_top, safe_mb, 0, keepdims=False)
        entering = jnp.where(segment_at == segments - 1, top_grad, received)
        mid_grad, grads_two = block_sharded(
            entering,
            take_micro(inputs_two, safe_mb),
            take_micro(conv_two, safe_mb),
            proj_weight[0, 1],
            conv_weight[0, 1],
            norm_gain[0, 1],
            norm_bias[0, 1],
        )
        out_grad, grads_one = block_sharded(
            mid_grad,
            take_micro(inputs_one, safe_mb),
            take_micro(conv_one, safe_mb),
            proj_weight[0, 0],
            conv_weight[0, 0],
            norm_gain[0, 0],
            norm_bias[0, 0],
        )
        weight_mask = is_valid.astype(jnp.float32)
        proj_acc = proj_acc + weight_mask * jnp.stack((grads_one[0], grads_two[0]))
        conv_acc = conv_acc + weight_mask * jnp.stack((grads_one[1], grads_two[1]))
        gain_acc = gain_acc + weight_mask * jnp.stack((grads_one[2], grads_two[2]))
        bias_acc = bias_acc + weight_mask * jnp.stack((grads_one[3], grads_two[3]))
        current = lax.dynamic_index_in_dim(latent[0], safe_mb, 0, keepdims=False)
        kept = jnp.where(is_valid, out_grad, current)
        latent = lax.dynamic_update_index_in_dim(latent, kept[None, None], safe_mb, 1)
        received = passed_along(out_grad, "segment", -1)
        return (received, latent, proj_acc, conv_acc, gain_acc, bias_acc)

    final = lax.fori_loop(0, ticks, one_tick, initial)
    latent = final[1]
    proj_sum, conv_sum, gain_sum, bias_sum = lax.psum(
        (final[2], final[3], final[4], final[5]), "dp"
    )
    return (latent, proj_sum[None], conv_sum[None], gain_sum[None], bias_sum[None])


def solution(mesh):
    return jax.shard_map(
        per_device,
        mesh=mesh,
        in_specs=(
            P("dp", None, "chan"),
            P("segment", "dp", "chan", None),
            P("segment", "dp", "chan", None),
            P("segment", "dp", "chan", None),
            P("segment", "dp", "chan", None),
            P("segment", None, "chan", None),
            P("segment", None, "chan", None),
            P("segment", None, "chan"),
            P("segment", None, "chan"),
        ),
        out_specs=(
            P("segment", "dp", None, "chan"),
            P("segment", None, "chan", None),
            P("segment", None, "chan", None),
            P("segment", None, "chan"),
            P("segment", None, "chan"),
        ),
        check_vma=False,
    )
```

profile of v0, /device:TPU:2, one launch (start us, length us, event | category | flops | bytes accessed | tf_op | source)
XLA Modules:
  0.0 469.4 jit_solution(2428649469921807830)
XLA Ops:
  7.3 1.8 copy.64
  9.6 357.8 %while.26 = (s32[]{:T(128)}, bf16[1536,16]{0,1:T(8,128)(2,1)S(1)}, bf16[1,1,1536,16]{2,3,1,0:T(8,128)(2,1)}, f32[2,96,1536]{2,1,0:T(8,128)S(1)}, f32[2,96,432]{1...) while((s32[]{:T(128)}, bf16[1536,16]{0,1:T(8,128)(2,1)S(1)}, ...), condition=%wide.region_21.22_spmd.clone, body=%wide.region_0.21_spmd.clone.sunk | while | flops 392720768 | bytes 27672152 | solution.py:158
  14.7 19.7 %all_gather.24 = bf16[1536,256]{0,1:T(8,128)(2,1)S(1)} all-gather(bf16[1536,16]{0,1:T(8,128)(2,1)S(1)} %bitcast_select_fusion.3), channel_id=1, replica_groups=mesh['segment'=4,'chan'=16,'dp'=8] {'chan'}, dimensions={1}, use_global_device_ids=true | all-gather | bytes 835584 | tf_op jit(solution)/shard_map/while/body/eval_jaxpr/all_gather | solution.py:81
  34.4 2.0 multiply_reduce_fusion.14
  40.7 4.4 all-to-all-start
  53.2 18.4 %all_gather.25 = bf16[1536,256]{0,1:T(8,128)(2,1)S(1)} all-gather(bf16[1536,16]{0,1:T(8,128)(2,1)S(1)} %add_convert_fusion.4), channel_id=1, replica_groups=mesh['segment'=4,'chan'=16,'dp'=8] {'chan'}, dimensions={1}, use_global_device_ids=true | all-gather | bytes 835584 | tf_op jit(solution)/shard_map/while/body/eval_jaxpr/all_gather | solution.py:81
  71.6 2.0 multiply_reduce_fusion.15
  76.8 4.6 all-to-all-start.1
  88.9 1.2 copy.167
  91.7 1.4 fusion.358
  93.2 3.9 collective-permute-start
  97.2 1.9 collective-permute-done
  104.2 19.4 %all_gather.24 = bf16[1536,256]{0,1:T(8,128)(2,1)S(1)} all-gather(bf16[1536,16]{0,1:T(8,128)(2,1)S(1)} %bitcast_select_fusion.3), channel_id=1, replica_groups=mesh['segment'=4,'chan'=16,'dp'=8] {'chan'}, dimensions={1}, use_global_device_ids=true | all-gather | bytes 835584 | tf_op jit(solution)/shard_map/while/body/eval_jaxpr/all_gather | solution.py:81
  123.6 2.0 multiply_reduce_fusion.14
  129.9 4.6 all-to-all-start
  141.4 1.0 all-to-all-done
  142.6 18.4 %all_gather.25 = bf16[1536,256]{0,1:T(8,128)(2,1)S(1)} all-gather(bf16[1536,16]{0,1:T(8,128)(2,1)S(1)} %add_convert_fusion.4), channel_id=1, replica_groups=mesh['segment'=4,'chan'=16,'dp'=8] {'chan'}, dimensions={1}, use_global_device_ids=true | all-gather | bytes 835584 | tf_op jit(solution)/shard_map/while/body/eval_jaxpr/all_gather | solution.py:81
  161.0 2.0 multiply_reduce_fusion.15
  166.3 4.6 all-to-all-start.1
  178.3 1.2 copy.167
  181.2 1.4 fusion.358
  182.6 3.9 collective-permute-start
  186.6 1.9 collective-permute-done
  193.7 19.4 %all_gather.24 = bf16[1536,256]{0,1:T(8,128)(2,1)S(1)} all-gather(bf16[1536,16]{0,1:T(8,128)(2,1)S(1)} %bitcast_select_fusion.3), channel_id=1, replica_groups=mesh['segment'=4,'chan'=16,'dp'=8] {'chan'}, dimensions={1}, use_global_device_ids=true | all-gather | bytes 835584 | tf_op jit(solution)/shard_map/while/body/eval_jaxpr/all_gather | solution.py:81
  213.1 2.0 multiply_reduce_fusion.14
  219.4 4.6 all-to-all-start
  230.9 1.0 all-to-all-done
  232.1 18.4 %all_gather.25 = bf16[1536,256]{0,1:T(8,128)(2,1)S(1)} all-gather(bf16[1536,16]{0,1:T(8,128)(2,1)S(1)} %add_convert_fusion.4), channel_id=1, replica_groups=mesh['segment'=4,'chan'=16,'dp'=8] {'chan'}, dimensions={1}, use_global_device_ids=true | all-gather | bytes 835584 | tf_op jit(solution)/shard_map/while/body/eval_jaxpr/all_gather | solution.py:81
  250.5 2.0 multiply_reduce_fusion.15
  255.7 4.6 all-to-all-start.1
  267.8 1.2 copy.167
  270.6 1.4 fusion.358
  272.1 3.9 collective-permute-start
  276.1 1.9 collective-permute-done
  283.1 19.4 %all_gather.24 = bf16[1536,256]{0,1:T(8,128)(2,1)S(1)} all-gather(bf16[1536,16]{0,1:T(8,128)(2,1)S(1)} %bitcast_select_fusion.3), channel_id=1, replica_groups=mesh['segment'=4,'chan'=16,'dp'=8] {'chan'}, dimensions={1}, use_global_device_ids=true | all-gather | bytes 835584 | tf_op jit(solution)/shard_map/while/body/eval_jaxpr/all_gather | solution.py:81
  302.5 2.0 multiply_reduce_fusion.14
  308.8 4.6 all-to-all-start
  321.5 18.4 %all_gather.25 = bf16[1536,256]{0,1:T(8,128)(2,1)S(1)} all-gather(bf16[1536,16]{0,1:T(8,128)(2,1)S(1)} %add_convert_fusion.4), channel_id=1, replica_groups=mesh['segment'=4,'chan'=16,'dp'=8] {'chan'}, dimensions={1}, use_global_device_ids=true | all-gather | bytes 835584 | tf_op jit(solution)/shard_map/while/body/eval_jaxpr/all_gather | solution.py:81
  339.9 2.0 multiply_reduce_fusion.15
  345.1 4.6 all-to-all-start.1
  357.2 1.2 copy.167
  360.0 1.4 fusion.358
  361.5 3.9 collective-permute-start
  365.5 1.9 collective-permute-done
  367.5 2.4 copy.65
  369.9 23.8 %all-reduce.18 = (f32[1,2,96]{2,1,0:T(2,128)}, f32[1,2,96]{2,1,0:T(2,128)}) all-reduce(f32[1,2,96]{2,1,0:T(2,128)S(1)} %bitcast.586, f32[1,2,96]{2,1,0:T(2,128)S(1)} %bitcast.587), channel_id=1, replica_groups=mesh['segment'=4,'chan'=16,'dp'=8] {'dp'}, use_global_device_ids=true, to_apply=%region_24.25 | all-reduce | flops 384 | bytes 3072 | tf_op jit(solution)/shard_map/psum | solution.py:160
  393.7 65.7 %all-reduce.22.cloned.1.call-done = (f32[1,2,96,1536]{3,2,1,0:T(8,128)}, f32[1,2,96,432]{3,2,1,0:T(8,128)}) async-done(((f32[1,2,96,1536]{3,2,1,0:T(8,128)}, f32[1,2,96,432]{3,2,1,0:T(8,128)}), (f32[1,2,96,1536]{3,2,1,0:T(8,128)}, f32[1,2,96,432]{3,2,1,0:T(8,128)})) %all-reduce.22.cloned.1.call-update) | async-done | bytes 1511440 | tf_op jit(solution)/shard_map/psum | solution.py:160
  459.4 2.4 copy.207
  (683 shorter events, 116.1 us)
Async XLA Ops:
  7.2 452.2 %all-reduce.22.cloned.1.call-start = ((), (), s32[]{:S(2)}) async-start(), calls=%async_computation.2 | async-start | bytes 3145728 | tf_op jit(solution)/shard_map/psum | solution.py:160
  9.7 29.8 %copy-start.30 = (pred[256]{0:T(512)(128)(4,1)}, pred[256]{0:T(512)(128)(4,1)S(1)}, u32[]{:S(2)}) copy-start(pred[256]{0:T(512)(128)(4,1)S(1)} %compare_and_fusion.7) | copy-start | bytes 772 | tf_op jit(solution)/shard_map/while
  9.7 29.8 %copy-start.27 = (pred[256]{0:T(512)(128)(4,1)}, pred[256]{0:T(512)(128)(4,1)S(1)}, u32[]{:S(2)}) copy-start(pred[256]{0:T(512)(128)(4,1)S(1)} %compare_and_fusion.8) | copy-start | bytes 772 | tf_op jit(solution)/shard_map/while
  39.5 9.8 %copy-start.7 = (bf16[1,1,96,256]{3,2,1,0:T(8,128)(2,1)S(1)}, bf16[1,1,96,256]{3,2,1,0:T(8,128)(2,1)}, u32[]{:S(2)}) copy-start(bf16[1,1,96,256]{3,2,1,0:T(8,128)(2,1)} %get-tuple-element.857) | copy-start | bytes 147460 | tf_op jit(solution)/shard_map/while
  39.8 9.5 %copy-start.31 = (pred[256]{0:T(512)(128)(4,1)S(1)}, pred[256]{0:T(512)(128)(4,1)}, u32[]{:S(2)}) copy-start(pred[256]{0:T(512)(128)(4,1)} %copy-done.30) | copy-start | bytes 772 | tf_op jit(solution)/shard_map/while
  39.8 9.9 %copy-start.28 = (pred[256]{0:T(512)(128)(4,1)S(1)}, pred[256]{0:T(512)(128)(4,1)}, u32[]{:S(2)}) copy-start(pred[256]{0:T(512)(128)(4,1)} %copy-done.27) | copy-start | bytes 772 | tf_op jit(solution)/shard_map/while
  40.7 12.3 %all-to-all-start = ((bf16[96,16,16]{0,2,1:T(8,128)(2,1)}), bf16[96,16,16]{0,2,1:T(8,128)(2,1)S(1)}, u32[]{:S(2)}, u32[]{:S(2)}) async-start(bf16[96,16,16]{0,2,1:T(8,128)(2,1)} %convert_element_type.430), calls=%async_computation | async-start | bytes 131072 | tf_op jit(solution)/shard_map/while/body/eval_jaxpr/all_to_all | solution.py:87
  52.0 19.6 %copy-start.22 = (f32[96]{0:T(128)S(1)}, f32[96]{0:T(128)}, u32[]{:S(2)}) copy-start(f32[96]{0:T(128)} %mul.953) | copy-start | bytes 1156 | tf_op jit(solution)/shard_map/while
  75.0 6.5 %copy-start.6 = (bf16[1,1,96,256]{3,2,1,0:T(8,128)(2,1)S(1)}, bf16[1,1,96,256]{3,2,1,0:T(8,128)(2,1)}, u32[]{:S(2)}) copy-start(bf16[1,1,96,256]{3,2,1,0:T(8,128)(2,1)} %get-tuple-element.856) | copy-start | bytes 147460 | tf_op jit(solution)/shard_map/while
  76.8 14.7 %all-to-all-start.1 = ((bf16[96,16,16]{0,2,1:T(8,128)(2,1)}), bf16[96,16,16]{0,2,1:T(8,128)(2,1)S(1)}, u32[]{:S(2)}, u32[]{:S(2)}) async-start(bf16[96,16,16]{0,2,1:T(8,128)(2,1)} %convert_element_type.431), calls=%async_computation.1 | async-start | bytes 131072 | tf_op jit(solution)/shard_map/while/body/eval_jaxpr/all_to_all | solution.py:87
  91.5 7.6 %copy-start.4 = (f32[2,96,432]{1,2,0:T(8,128)}, f32[2,96,432]{1,2,0:T(8,128)S(1)}, u32[]{:S(2)}) copy-start(f32[2,96,432]{1,2,0:T(8,128)S(1)} %fusion.378) | copy-start | bytes 995332 | tf_op jit(solution)/shard_map/while
  93.2 6.0 %collective-permute-start = (bf16[1536,16]{0,1:T(8,128)(2,1)S(1)}, bf16[1536,16]{0,1:T(8,128)(2,1)S(1)}, u32[]{:S(2)}, u32[]{:S(2)}) collective-permute-start(bf16[1536,16]{0,1:T(8,128)(2,1)S(1)} %get-tuple-element.790), channel_id=1, source_target_pairs={{128,0},{256,128},{384,256},{129,1},{257,129},{385,257},{130,2},{2... | collective-permute-start | bytes 147464 | tf_op jit(solution)/shard_map/while/body/eval_jaxpr/ppermute | solution.py:14
  99.2 29.5 %copy-start.30 = (pred[256]{0:T(512)(128)(4,1)}, pred[256]{0:T(512)(128)(4,1)S(1)}, u32[]{:S(2)}) copy-start(pred[256]{0:T(512)(128)(4,1)S(1)} %compare_and_fusion.7) | copy-start | bytes 772 | tf_op jit(solution)/shard_map/while
  99.2 29.5 %copy-start.27 = (pred[256]{0:T(512)(128)(4,1)}, pred[256]{0:T(512)(128)(4,1)S(1)}, u32[]{:S(2)}) copy-start(pred[256]{0:T(512)(128)(4,1)S(1)} %compare_and_fusion.8) | copy-start | bytes 772 | tf_op jit(solution)/shard_map/while
  128.0 6.5 %copy-start.2 = (bf16[1,1,96,256]{3,2,1,0:T(8,128)(2,1)S(1)}, bf16[1,1,96,256]{3,2,1,0:T(8,128)(2,1)}, u32[]{:S(2)}) copy-start(bf16[1,1,96,256]{3,2,1,0:T(8,128)(2,1)} %get-tuple-element.854) | copy-start | bytes 147460 | tf_op jit(solution)/shard_map/while
  128.7 10.0 %copy-start.7 = (bf16[1,1,96,256]{3,2,1,0:T(8,128)(2,1)S(1)}, bf16[1,1,96,256]{3,2,1,0:T(8,128)(2,1)}, u32[]{:S(2)}) copy-start(bf16[1,1,96,256]{3,2,1,0:T(8,128)(2,1)} %get-tuple-element.857) | copy-start | bytes 147460 | tf_op jit(solution)/shard_map/while
  129.0 9.7 %copy-start.31 = (pred[256]{0:T(512)(128)(4,1)S(1)}, pred[256]{0:T(512)(128)(4,1)}, u32[]{:S(2)}) copy-start(pred[256]{0:T(512)(128)(4,1)} %copy-done.30) | copy-start | bytes 772 | tf_op jit(solution)/shard_map/while
  129.0 10.1 %copy-start.28 = (pred[256]{0:T(512)(128)(4,1)S(1)}, pred[256]{0:T(512)(128)(4,1)}, u32[]{:S(2)}) copy-start(pred[256]{0:T(512)(128)(4,1)} %copy-done.27) | copy-start | bytes 772 | tf_op jit(solution)/shard_map/while
  129.9 12.5 %all-to-all-start = ((bf16[96,16,16]{0,2,1:T(8,128)(2,1)}), bf16[96,16,16]{0,2,1:T(8,128)(2,1)S(1)}, u32[]{:S(2)}, u32[]{:S(2)}) async-start(bf16[96,16,16]{0,2,1:T(8,128)(2,1)} %convert_element_type.430), calls=%async_computation | async-start | bytes 131072 | tf_op jit(solution)/shard_map/while/body/eval_jaxpr/all_to_all | solution.py:87
  141.4 19.6 %copy-start.22 = (f32[96]{0:T(128)S(1)}, f32[96]{0:T(128)}, u32[]{:S(2)}) copy-start(f32[96]{0:T(128)} %mul.953) | copy-start | bytes 1156 | tf_op jit(solution)/shard_map/while
  164.4 6.5 %copy-start.6 = (bf16[1,1,96,256]{3,2,1,0:T(8,128)(2,1)S(1)}, bf16[1,1,96,256]{3,2,1,0:T(8,128)(2,1)}, u32[]{:S(2)}) copy-start(bf16[1,1,96,256]{3,2,1,0:T(8,128)(2,1)} %get-tuple-element.856) | copy-start | bytes 147460 | tf_op jit(solution)/shard_map/while
  166.3 14.7 %all-to-all-start.1 = ((bf16[96,16,16]{0,2,1:T(8,128)(2,1)}), bf16[96,16,16]{0,2,1:T(8,128)(2,1)S(1)}, u32[]{:S(2)}, u32[]{:S(2)}) async-start(bf16[96,16,16]{0,2,1:T(8,128)(2,1)} %convert_element_type.431), calls=%async_computation.1 | async-start | bytes 131072 | tf_op jit(solution)/shard_map/while/body/eval_jaxpr/all_to_all | solution.py:87
  181.0 7.6 %copy-start.4 = (f32[2,96,432]{1,2,0:T(8,128)}, f32[2,96,432]{1,2,0:T(8,128)S(1)}, u32[]{:S(2)}) copy-start(f32[2,96,432]{1,2,0:T(8,128)S(1)} %fusion.378) | copy-start | bytes 995332 | tf_op jit(solution)/shard_map/while
  182.6 6.0 %collective-permute-start = (bf16[1536,16]{0,1:T(8,128)(2,1)S(1)}, bf16[1536,16]{0,1:T(8,128)(2,1)S(1)}, u32[]{:S(2)}, u32[]{:S(2)}) collective-permute-start(bf16[1536,16]{0,1:T(8,128)(2,1)S(1)} %get-tuple-element.790), channel_id=1, source_target_pairs={{128,0},{256,128},{384,256},{129,1},{257,129},{385,257},{130,2},{2... | collective-permute-start | bytes 147464 | tf_op jit(solution)/shard_map/while/body/eval_jaxpr/ppermute | solution.py:14
  188.6 29.5 %copy-start.30 = (pred[256]{0:T(512)(128)(4,1)}, pred[256]{0:T(512)(128)(4,1)S(1)}, u32[]{:S(2)}) copy-start(pred[256]{0:T(512)(128)(4,1)S(1)} %compare_and_fusion.7) | copy-start | bytes 772 | tf_op jit(solution)/shard_map/while
  188.7 29.5 %copy-start.27 = (pred[256]{0:T(512)(128)(4,1)}, pred[256]{0:T(512)(128)(4,1)S(1)}, u32[]{:S(2)}) copy-start(pred[256]{0:T(512)(128)(4,1)S(1)} %compare_and_fusion.8) | copy-start | bytes 772 | tf_op jit(solution)/shard_map/while
  217.5 6.5 %copy-start.2 = (bf16[1,1,96,256]{3,2,1,0:T(8,128)(2,1)S(1)}, bf16[1,1,96,256]{3,2,1,0:T(8,128)(2,1)}, u32[]{:S(2)}) copy-start(bf16[1,1,96,256]{3,2,1,0:T(8,128)(2,1)} %get-tuple-element.854) | copy-start | bytes 147460 | tf_op jit(solution)/shard_map/while
  218.2 10.0 %copy-start.7 = (bf16[1,1,96,256]{3,2,1,0:T(8,128)(2,1)S(1)}, bf16[1,1,96,256]{3,2,1,0:T(8,128)(2,1)}, u32[]{:S(2)}) copy-start(bf16[1,1,96,256]{3,2,1,0:T(8,128)(2,1)} %get-tuple-element.857) | copy-start | bytes 147460 | tf_op jit(solution)/shard_map/while
  218.5 9.7 %copy-start.31 = (pred[256]{0:T(512)(128)(4,1)S(1)}, pred[256]{0:T(512)(128)(4,1)}, u32[]{:S(2)}) copy-start(pred[256]{0:T(512)(128)(4,1)} %copy-done.30) | copy-start | bytes 772 | tf_op jit(solution)/shard_map/while
  218.5 10.1 %copy-start.28 = (pred[256]{0:T(512)(128)(4,1)S(1)}, pred[256]{0:T(512)(128)(4,1)}, u32[]{:S(2)}) copy-start(pred[256]{0:T(512)(128)(4,1)} %copy-done.27) | copy-start | bytes 772 | tf_op jit(solution)/shard_map/while
  219.4 12.5 %all-to-all-start = ((bf16[96,16,16]{0,2,1:T(8,128)(2,1)}), bf16[96,16,16]{0,2,1:T(8,128)(2,1)S(1)}, u32[]{:S(2)}, u32[]{:S(2)}) async-start(bf16[96,16,16]{0,2,1:T(8,128)(2,1)} %convert_element_type.430), calls=%async_computation | async-start | bytes 131072 | tf_op jit(solution)/shard_map/while/body/eval_jaxpr/all_to_all | solution.py:87
  230.9 19.6 %copy-start.22 = (f32[96]{0:T(128)S(1)}, f32[96]{0:T(128)}, u32[]{:S(2)}) copy-start(f32[96]{0:T(128)} %mul.953) | copy-start | bytes 1156 | tf_op jit(solution)/shard_map/while
  253.8 6.5 %copy-start.6 = (bf16[1,1,96,256]{3,2,1,0:T(8,128)(2,1)S(1)}, bf16[1,1,96,256]{3,2,1,0:T(8,128)(2,1)}, u32[]{:S(2)}) copy-start(bf16[1,1,96,256]{3,2,1,0:T(8,128)(2,1)} %get-tuple-element.856) | copy-start | bytes 147460 | tf_op jit(solution)/shard_map/while
  255.7 14.7 %all-to-all-start.1 = ((bf16[96,16,16]{0,2,1:T(8,128)(2,1)}), bf16[96,16,16]{0,2,1:T(8,128)(2,1)S(1)}, u32[]{:S(2)}, u32[]{:S(2)}) async-start(bf16[96,16,16]{0,2,1:T(8,128)(2,1)} %convert_element_type.431), calls=%async_computation.1 | async-start | bytes 131072 | tf_op jit(solution)/shard_map/while/body/eval_jaxpr/all_to_all | solution.py:87
  270.4 7.6 %copy-start.4 = (f32[2,96,432]{1,2,0:T(8,128)}, f32[2,96,432]{1,2,0:T(8,128)S(1)}, u32[]{:S(2)}) copy-start(f32[2,96,432]{1,2,0:T(8,128)S(1)} %fusion.378) | copy-start | bytes 995332 | tf_op jit(solution)/shard_map/while
  272.1 6.0 %collective-permute-start = (bf16[1536,16]{0,1:T(8,128)(2,1)S(1)}, bf16[1536,16]{0,1:T(8,128)(2,1)S(1)}, u32[]{:S(2)}, u32[]{:S(2)}) collective-permute-start(bf16[1536,16]{0,1:T(8,128)(2,1)S(1)} %get-tuple-element.790), channel_id=1, source_target_pairs={{128,0},{256,128},{384,256},{129,1},{257,129},{385,257},{130,2},{2... | collective-permute-start | bytes 147464 | tf_op jit(solution)/shard_map/while/body/eval_jaxpr/ppermute | solution.py:14
  278.1 29.5 %copy-start.30 = (pred[256]{0:T(512)(128)(4,1)}, pred[256]{0:T(512)(128)(4,1)S(1)}, u32[]{:S(2)}) copy-start(pred[256]{0:T(512)(128)(4,1)S(1)} %compare_and_fusion.7) | copy-start | bytes 772 | tf_op jit(solution)/shard_map/while
  278.1 29.5 %copy-start.27 = (pred[256]{0:T(512)(128)(4,1)}, pred[256]{0:T(512)(128)(4,1)S(1)}, u32[]{:S(2)}) copy-start(pred[256]{0:T(512)(128)(4,1)S(1)} %compare_and_fusion.8) | copy-start | bytes 772 | tf_op jit(solution)/shard_map/while
  306.9 6.5 %copy-start.2 = (bf16[1,1,96,256]{3,2,1,0:T(8,128)(2,1)S(1)}, bf16[1,1,96,256]{3,2,1,0:T(8,128)(2,1)}, u32[]{:S(2)}) copy-start(bf16[1,1,96,256]{3,2,1,0:T(8,128)(2,1)} %get-tuple-element.854) | copy-start | bytes 147460 | tf_op jit(solution)/shard_map/while
  307.6 10.0 %copy-start.7 = (bf16[1,1,96,256]{3,2,1,0:T(8,128)(2,1)S(1)}, bf16[1,1,96,256]{3,2,1,0:T(8,128)(2,1)}, u32[]{:S(2)}) copy-start(bf16[1,1,96,256]{3,2,1,0:T(8,128)(2,1)} %get-tuple-element.857) | copy-start | bytes 147460 | tf_op jit(solution)/shard_map/while
  307.9 9.7 %copy-start.31 = (pred[256]{0:T(512)(128)(4,1)S(1)}, pred[256]{0:T(512)(128)(4,1)}, u32[]{:S(2)}) copy-start(pred[256]{0:T(512)(128)(4,1)} %copy-done.30) | copy-start | bytes 772 | tf_op jit(solution)/shard_map/while
  307.9 10.1 %copy-start.28 = (pred[256]{0:T(512)(128)(4,1)S(1)}, pred[256]{0:T(512)(128)(4,1)}, u32[]{:S(2)}) copy-start(pred[256]{0:T(512)(128)(4,1)} %copy-done.27) | copy-start | bytes 772 | tf_op jit(solution)/shard_map/while
  308.8 12.5 %all-to-all-start = ((bf16[96,16,16]{0,2,1:T(8,128)(2,1)}), bf16[96,16,16]{0,2,1:T(8,128)(2,1)S(1)}, u32[]{:S(2)}, u32[]{:S(2)}) async-start(bf16[96,16,16]{0,2,1:T(8,128)(2,1)} %convert_element_type.430), calls=%async_computation | async-start | bytes 131072 | tf_op jit(solution)/shard_map/while/body/eval_jaxpr/all_to_all | solution.py:87
  320.3 19.6 %copy-start.22 = (f32[96]{0:T(128)S(1)}, f32[96]{0:T(128)}, u32[]{:S(2)}) copy-start(f32[96]{0:T(128)} %mul.953) | copy-start | bytes 1156 | tf_op jit(solution)/shard_map/while
  343.3 6.5 %copy-start.6 = (bf16[1,1,96,256]{3,2,1,0:T(8,128)(2,1)S(1)}, bf16[1,1,96,256]{3,2,1,0:T(8,128)(2,1)}, u32[]{:S(2)}) copy-start(bf16[1,1,96,256]{3,2,1,0:T(8,128)(2,1)} %get-tuple-element.856) | copy-start | bytes 147460 | tf_op jit(solution)/shard_map/while
  345.1 14.7 %all-to-all-start.1 = ((bf16[96,16,16]{0,2,1:T(8,128)(2,1)}), bf16[96,16,16]{0,2,1:T(8,128)(2,1)S(1)}, u32[]{:S(2)}, u32[]{:S(2)}) async-start(bf16[96,16,16]{0,2,1:T(8,128)(2,1)} %convert_element_type.431), calls=%async_computation.1 | async-start | bytes 131072 | tf_op jit(solution)/shard_map/while/body/eval_jaxpr/all_to_all | solution.py:87
  359.8 7.6 %copy-start.4 = (f32[2,96,432]{1,2,0:T(8,128)}, f32[2,96,432]{1,2,0:T(8,128)S(1)}, u32[]{:S(2)}) copy-start(f32[2,96,432]{1,2,0:T(8,128)S(1)} %fusion.378) | copy-start | bytes 995332 | tf_op jit(solution)/shard_map/while
  361.5 6.0 %collective-permute-start = (bf16[1536,16]{0,1:T(8,128)(2,1)S(1)}, bf16[1536,16]{0,1:T(8,128)(2,1)S(1)}, u32[]{:S(2)}, u32[]{:S(2)}) collective-permute-start(bf16[1536,16]{0,1:T(8,128)(2,1)S(1)} %get-tuple-element.790), channel_id=1, source_target_pairs={{128,0},{256,128},{384,256},{129,1},{257,129},{385,257},{130,2},{2... | collective-permute-start | bytes 147464 | tf_op jit(solution)/shard_map/while/body/eval_jaxpr/ppermute | solution.py:14
  (85 other events, 262.7 us)
Sparse Core Ops, SparseCore 0:
  370.0 89.2 all-reduce.21
where the time goes:
time: 472 us; the launch traced here: 469 us
  blocking collectives  175 us (37%)
  waiting for transfers between devices  77.5 us (16%)
  matrix products  66.1 us (14%)
  local copies, waits for them, and re-layouts  56 us (12%)
  starting transfers between devices  52.6 us (11%)
  other arithmetic  25.2 us (5%)
  between operations  14.1 us (3%)
    all_gather x8, blocking collectives, block_sharded(): grad_piece = lax.all_gather(grad_slab, 'chan', axis=1, tiled=True)  152 us
    psum x1, waiting for transfers between devices, per_device(): lax.psum((final[2], final[3], final[4], final[5]), 'dp')  65.7 us
    dot_general x72, matrix products, conv_backward(): jnp.einsum('gop,gjp->goj', grad_pre, source, preferred_element_type=jnp.f...  36.9 us
    all_to_all x8, starting transfers between devices, block_sharded(): lax.all_to_all(branch, 'chan', split_axis=1, concat_axis=0, tiled=True)  36.9 us
    psum x1, blocking collectives, per_device(): lax.psum((final[2], final[3], final[4], final[5]), 'dp')  23.8 us
    dot_general x8, matrix products, block_sharded(): fresh = jnp.dot(w_proj, grad_piece, preferred_element_type=jnp.float32)  16 us
    ppermute x4, starting transfers between devices, passed_along(): return lax.ppermute(block, axis, route)  15.7 us
    dot_general x72, matrix products, conv_backward(): jnp.einsum('goj,gop->gjp', taps_w[:, :, tap_at, :], grad_pre, preferred_e...  10.6 us
  transfers between devices with their start and end apart: 13, of which 9 were waited for; matrix products, arithmetic and copies ran while one was open for 13% of the time, Pallas kernels for 0%

commit v1 on v0

--- a/solution.py
+++ b/solution.py
@@ -78,7 +78,16 @@
 def block_sharded(grad_slab, saved_in, saved_pre, w_proj, w_conv, gain_vec, bias_vec):
     norm_state = norm_forward(saved_pre, gain_vec, bias_vec)
     act_bf = norm_state[5]
-    grad_piece = lax.all_gather(grad_slab, "chan", axis=1, tiled=True)
+    ways = lax.axis_size("chan")
+    up = [(d, (d + 1) % ways) for d in range(ways)]
+    down = [(d, (d - 1) % ways) for d in range(ways)]
+    earlier, later = ([grad_slab], [grad_slab])
+    for __2 in range(ways // 2):
+        earlier.append(lax.ppermute(earlier[-1], "chan", up))
+    for __2 in range((ways - 1) // 2):
+        later.append(lax.ppermute(later[-1], "chan", down))
+    line = jnp.concatenate([*earlier[::-1], *later[1:]], axis=1)
+    grad_piece = jnp.roll(line, (lax.axis_index("chan") - ways // 2) * grad_slab.shape[1], axis=1)
     fresh = jnp.dot(w_proj, grad_piece, preferred_element_type=jnp.float32)
     weight_acc = lax.dot_general(
         act_bf, grad_piece, (((1,), (1,)), ((), ())), preferred_element_type=jnp.float32

time: 472 us -> 636 us (1.35)
  starting transfers between devices: 52.6 us -> 222 us
  blocking collectives: 175 us -> 23.3 us
  waiting for transfers between devices: 77.5 us -> 222 us
  matrix products: 66.1 us -> 47.3 us
  local copies, waits for them, and re-layouts: 56 us -> 68.1 us
    ppermute x0 -> x120, starting transfers between devices: none -> 168 us  [the longest x56 166 us: block_sharded(): later.append(lax.ppermute(later[-1], 'chan', down))]
    all_gather x8 -> x0, blocking collectives: 152 us -> none  [block_sharded(): grad_piece = lax.all_gather(grad_slab, 'chan', axis=1, tiled=True)]
    ppermute x0 -> x120, waiting for transfers between devices: none -> 108 us  [the longest x64 96.9 us: block_sharded(): earlier.append(lax.ppermute(earlier[-1], 'chan', up))]
    all_to_all x8, waiting for transfers between devices: 4.02 us -> 45 us  [block_sharded(): lax.all_to_all(branch, 'chan', split_axis=1, concat_axis=0, tiled=True)]
    dot_general x72, matrix products: 36.9 us -> 14.3 us  [conv_backward(): jnp.einsum('gop,gjp->goj', grad_pre, source, preferred_element_type=jnp.f...]
    while x232 -> x552, local copies, waits for them, and re-layouts: 4.38 us -> 25.4 us
    dot_general x8, matrix products: 2.62 us -> 12.4 us  [block_sharded(): lax.dot_general(act_bf, grad_piece, (((1,), (1,)), ((), ())), preferred_e...]
  transfers between devices with their start and end apart: 13 -> 133, of which waited for: 9 -> 81; matrix products, arithmetic and copies ran while one was open for 13% -> 14% of each run, Pallas kernels for 0% -> 0%
where the time goes in v1:
time: 636 us; the launch traced here: 632 us
  starting transfers between devices  222 us (35%)
  waiting for transfers between devices  222 us (35%)
  local copies, waits for them, and re-layouts  68.1 us (11%)
  matrix products  47.3 us (7%)
  other arithmetic  30.4 us (5%)
  blocking collectives  23.3 us (4%)
  between operations  14.1 us (2%)
    ppermute x56, starting transfers between devices, block_sharded(): later.append(lax.ppermute(later[-1], 'chan', down))  166 us
    ppermute x64, waiting for transfers between devices, block_sharded(): earlier.append(lax.ppermute(earlier[-1], 'chan', up))  96.9 us
    psum x1, waiting for transfers between devices, per_device(): lax.psum((final[2], final[3], final[4], final[5]), 'dp')  61.8 us
    all_to_all x8, waiting for transfers between devices, block_sharded(): lax.all_to_all(branch, 'chan', split_axis=1, concat_axis=0, tiled=True)  45 us
    all_to_all x8, starting transfers between devices, block_sharded(): lax.all_to_all(branch, 'chan', split_axis=1, concat_axis=0, tiled=True)  37.1 us
    while x552, local copies, waits for them, and re-layouts  25.4 us
    psum x1, blocking collectives, per_device(): lax.psum((final[2], final[3], final[4], final[5]), 'dp')  23.3 us
    ppermute x4, starting transfers between devices, passed_along(): return lax.ppermute(block, axis, route)  17.5 us
  transfers between devices with their start and end apart: 133, of which 81 were waited for; matrix products, arithmetic and copies ran while one was open for 14% of the time, Pallas kernels for 0%

profile of v1, /device:TPU:2, one launch (start us, length us, event | category | flops | bytes accessed | tf_op | source)
XLA Modules:
  0.0 631.7 jit_solution(10341750229059243562)
XLA Ops:
  9.6 525.8 %while.26 = (s32[]{:T(128)}, bf16[1536,16]{0,1:T(8,128)(2,1)S(1)}, bf16[1,1,1536,16]{2,3,1,0:T(8,128)(2,1)}, f32[2,96,1536]{2,1,0:T(8,128)S(1)}, f32[2,96,432]{1...) while((s32[]{:T(128)}, bf16[1536,16]{0,1:T(8,128)(2,1)S(1)}, ...), condition=%wide.region_21.23_spmd.clone, body=%wide.region_0.22_spmd.clone.sunk | while | flops 399012256 | bytes 44390616 | solution.py:167
  20.2 4.3 collective-permute-done.1
  34.5 3.0 collective-permute-start.11
  39.3 3.0 collective-permute-start.12
  44.0 3.0 collective-permute-start.13
  58.7 7.5 %all-to-all-start = ((bf16[96,16,16]{0,2,1:T(8,128)(2,1)}), bf16[96,16,16]{0,2,1:T(8,128)(2,1)S(1)}, u32[]{:S(2)}, u32[]{:S(2)}) async-start(bf16[96,16,16]{0,2,1:T(8,128)(2,1)} %convert_element_type.430), calls=%async_computation | async-start | bytes 131072 | tf_op jit(solution)/shard_map/while/body/eval_jaxpr/all_to_all | solution.py:96
  66.7 7.4 %all-to-all-done = bf16[96,16,16]{0,2,1:T(8,128)(2,1)S(1)} async-done(((bf16[96,16,16]{0,2,1:T(8,128)(2,1)}), bf16[96,16,16]{0,2,1:T(8,128)(2,1)S(1)}, u32[]{:S(2)}, u32[]{:S(2)}) %all-to-all-start) | async-done | bytes 49184 | tf_op jit(solution)/shard_map/while/body/eval_jaxpr/all_to_all | solution.py:96
  74.9 4.2 collective-permute-done.15
  84.0 3.0 collective-permute-start.24
  102.9 3.1 collective-permute-start.28
  124.3 4.1 all-to-all-start.1
  132.4 3.8 all-to-all-done.1
  137.3 4.7 collective-permute-start.30
  154.3 4.3 collective-permute-done.1
  168.7 3.0 collective-permute-start.11
  173.4 3.0 collective-permute-start.12
  178.1 3.0 collective-permute-start.13
  192.9 4.4 all-to-all-start
  197.7 7.4 %all-to-all-done = bf16[96,16,16]{0,2,1:T(8,128)(2,1)S(1)} async-done(((bf16[96,16,16]{0,2,1:T(8,128)(2,1)}), bf16[96,16,16]{0,2,1:T(8,128)(2,1)S(1)}, u32[]{:S(2)}, u32[]{:S(2)}) %all-to-all-start) | async-done | bytes 49184 | tf_op jit(solution)/shard_map/while/body/eval_jaxpr/all_to_all | solution.py:96
  205.9 4.2 collective-permute-done.15
  215.0 3.0 collective-permute-start.24
  233.9 3.1 collective-permute-start.28
  255.3 4.1 all-to-all-start.1
  263.4 3.8 all-to-all-done.1
  268.3 4.3 collective-permute-start.30
  284.9 4.3 collective-permute-done.1
  299.2 3.0 collective-permute-start.11
  304.0 3.0 collective-permute-start.12
  308.7 3.0 collective-permute-start.13
  323.4 4.4 all-to-all-start
  328.3 7.4 %all-to-all-done = bf16[96,16,16]{0,2,1:T(8,128)(2,1)S(1)} async-done(((bf16[96,16,16]{0,2,1:T(8,128)(2,1)}), bf16[96,16,16]{0,2,1:T(8,128)(2,1)S(1)}, u32[]{:S(2)}, u32[]{:S(2)}) %all-to-all-start) | async-done | bytes 49184 | tf_op jit(solution)/shard_map/while/body/eval_jaxpr/all_to_all | solution.py:96
  336.4 4.2 collective-permute-done.15
  345.5 3.0 collective-permute-start.24
  364.5 3.1 collective-permute-start.28
  385.8 4.1 all-to-all-start.1
  394.0 3.8 all-to-all-done.1
  398.9 4.3 collective-permute-start.30
  415.5 4.3 collective-permute-done.1
  429.8 3.0 collective-permute-start.11
  454.0 4.4 all-to-all-start
  458.8 7.4 %all-to-all-done = bf16[96,16,16]{0,2,1:T(8,128)(2,1)S(1)} async-done(((bf16[96,16,16]{0,2,1:T(8,128)(2,1)}), bf16[96,16,16]{0,2,1:T(8,128)(2,1)S(1)}, u32[]{:S(2)}, u32[]{:S(2)}) %all-to-all-start) | async-done | bytes 49184 | tf_op jit(solution)/shard_map/while/body/eval_jaxpr/all_to_all | solution.py:96
  467.0 4.2 collective-permute-done.15
  495.1 3.1 collective-permute-start.28
  516.4 4.1 all-to-all-start.1
  524.6 3.8 all-to-all-done.1
  529.4 4.3 collective-permute-start.30
  536.6 23.3 %all-reduce.18 = (f32[1,2,96]{2,1,0:T(2,128)}, f32[1,2,96]{2,1,0:T(2,128)}) all-reduce(f32[1,2,96]{2,1,0:T(2,128)S(1)} %bitcast.574, f32[1,2,96]{2,1,0:T(2,128)S(1)} %bitcast.575), channel_id=1, replica_groups=mesh['segment'=4,'chan'=16,'dp'=8] {'dp'}, use_global_device_ids=true, to_apply=%region_24.26 | all-reduce | flops 384 | bytes 3072 | tf_op jit(solution)/shard_map/psum | solution.py:169
  559.9 61.8 %all-reduce.22.cloned.1.call-done = (f32[1,2,96,1536]{3,2,1,0:T(8,128)}, f32[1,2,96,432]{3,2,1,0:T(8,128)}) async-done(((f32[1,2,96,1536]{3,2,1,0:T(8,128)}, f32[1,2,96,432]{3,2,1,0:T(8,128)}), (f32[1,2,96,1536]{3,2,1,0:T(8,128)}, f32[1,2,96,432]{3,2,1,0:T(8,128)})) %all-reduce.22.cloned.1.call-update) | async-done | bytes 1511440 | tf_op jit(solution)/shard_map/psum | solution.py:169
  (1239 shorter events, 343.5 us)
Async XLA Ops:
  7.2 614.5 %all-reduce.22.cloned.1.call-start = ((), (), s32[]{:S(2)}) async-start(), calls=%async_computation.2 | async-start | bytes 3145728 | tf_op jit(solution)/shard_map/psum | solution.py:169
  10.5 9.3 %collective-permute-start = (bf16[1536,16]{0,1:T(8,128)(2,1)S(1)}, bf16[1536,16]{0,1:T(8,128)(2,1)S(1)}, u32[]{:S(2)}, u32[]{:S(2)}) collective-permute-start(bf16[1536,16]{0,1:T(8,128)(2,1)S(1)} %bitcast_select_fusion.3), channel_id=1, source_target_pairs={{0,8},{8,16},{16,24},{24,32},{32,40},{40,48},{48,56},{56,64},{64,7... | collective-permute-start | bytes 147464 | tf_op jit(solution)/shard_map/while/body/eval_jaxpr/ppermute | solution.py:86
  10.5 14.1 %collective-permute-start.8 = (bf16[1536,16]{0,1:T(8,128)(2,1)S(1)}, bf16[1536,16]{0,1:T(8,128)(2,1)S(1)}, u32[]{:S(2)}, u32[]{:S(2)}) collective-permute-start(bf16[1536,16]{0,1:T(8,128)(2,1)S(1)} %bitcast_select_fusion.3), channel_id=1, source_target_pairs={{0,120},{8,0},{16,8},{24,16},{32,24},{40,32},{48,40},{56,48},{64,5... | collective-permute-start | bytes 147464 | tf_op jit(solution)/shard_map/while/body/eval_jaxpr/ppermute | solution.py:88
  24.5 5.3 collective-permute-start.9
  44.0 6.0 collective-permute-start.13
  48.1 4.7 collective-permute-start.7
  58.7 15.4 %all-to-all-start = ((bf16[96,16,16]{0,2,1:T(8,128)(2,1)}), bf16[96,16,16]{0,2,1:T(8,128)(2,1)S(1)}, u32[]{:S(2)}, u32[]{:S(2)}) async-start(bf16[96,16,16]{0,2,1:T(8,128)(2,1)} %convert_element_type.430), calls=%async_computation | async-start | bytes 131072 | tf_op jit(solution)/shard_map/while/body/eval_jaxpr/all_to_all | solution.py:96
  102.7 4.8 collective-permute-start.21
  102.9 7.0 %collective-permute-start.28 = (bf16[1536,16]{0,1:T(8,128)(2,1)}, bf16[1536,16]{0,1:T(8,128)(2,1)}, u32[]{:S(2)}, u32[]{:S(2)}) collective-permute-start(bf16[1536,16]{0,1:T(8,128)(2,1)} %collective-permute-done.27), channel_id=1, source_target_pairs={{0,120},{8,0},{16,8},{24,16},{32,24},{40,32},{48,40},{56,48},{64,5... | collective-permute-start | bytes 147464 | tf_op jit(solution)/shard_map/while/body/eval_jaxpr/ppermute | solution.py:88
  107.6 5.3 collective-permute-start.22
  110.0 8.7 %collective-permute-start.29 = (bf16[1536,16]{0,1:T(8,128)(2,1)}, bf16[1536,16]{0,1:T(8,128)(2,1)S(1)}, u32[]{:S(2)}, u32[]{:S(2)}) collective-permute-start(bf16[1536,16]{0,1:T(8,128)(2,1)} %collective-permute-done.28), channel_id=1, source_target_pairs={{0,120},{8,0},{16,8},{24,16},{32,24},{40,32},{48,40},{56,48},{64,5... | collective-permute-start | bytes 147464 | tf_op jit(solution)/shard_map/while/body/eval_jaxpr/ppermute | solution.py:88
  124.3 12.0 %all-to-all-start.1 = ((bf16[96,16,16]{0,2,1:T(8,128)(2,1)}), bf16[96,16,16]{0,2,1:T(8,128)(2,1)}, u32[]{:S(2)}, u32[]{:S(2)}) async-start(bf16[96,16,16]{0,2,1:T(8,128)(2,1)} %convert_element_type.431), calls=%async_computation.1 | async-start | bytes 131072 | tf_op jit(solution)/shard_map/while/body/eval_jaxpr/all_to_all | solution.py:96
  137.3 6.4 %collective-permute-start.30 = (bf16[1536,16]{0,1:T(8,128)(2,1)S(1)}, bf16[1536,16]{0,1:T(8,128)(2,1)S(1)}, u32[]{:S(2)}, u32[]{:S(2)}) collective-permute-start(bf16[1536,16]{0,1:T(8,128)(2,1)S(1)} %get-tuple-element.792), channel_id=1, source_target_pairs={{128,0},{256,128},{384,256},{129,1},{257,129},{385,257},{130,2},{2... | collective-permute-start | bytes 147464 | tf_op jit(solution)/shard_map/while/body/eval_jaxpr/ppermute | solution.py:14
  144.6 9.3 %collective-permute-start = (bf16[1536,16]{0,1:T(8,128)(2,1)S(1)}, bf16[1536,16]{0,1:T(8,128)(2,1)S(1)}, u32[]{:S(2)}, u32[]{:S(2)}) collective-permute-start(bf16[1536,16]{0,1:T(8,128)(2,1)S(1)} %bitcast_select_fusion.3), channel_id=1, source_target_pairs={{0,8},{8,16},{16,24},{24,32},{32,40},{40,48},{48,56},{56,64},{64,7... | collective-permute-start | bytes 147464 | tf_op jit(solution)/shard_map/while/body/eval_jaxpr/ppermute | solution.py:86
  144.6 14.1 %collective-permute-start.8 = (bf16[1536,16]{0,1:T(8,128)(2,1)S(1)}, bf16[1536,16]{0,1:T(8,128)(2,1)S(1)}, u32[]{:S(2)}, u32[]{:S(2)}) collective-permute-start(bf16[1536,16]{0,1:T(8,128)(2,1)S(1)} %bitcast_select_fusion.3), channel_id=1, source_target_pairs={{0,120},{8,0},{16,8},{24,16},{32,24},{40,32},{48,40},{56,48},{64,5... | collective-permute-start | bytes 147464 | tf_op jit(solution)/shard_map/while/body/eval_jaxpr/ppermute | solution.py:88
  158.7 5.3 collective-permute-start.9
  178.1 6.0 collective-permute-start.13
  182.3 4.7 collective-permute-start.7
  192.9 12.2 %all-to-all-start = ((bf16[96,16,16]{0,2,1:T(8,128)(2,1)}), bf16[96,16,16]{0,2,1:T(8,128)(2,1)S(1)}, u32[]{:S(2)}, u32[]{:S(2)}) async-start(bf16[96,16,16]{0,2,1:T(8,128)(2,1)} %convert_element_type.430), calls=%async_computation | async-start | bytes 131072 | tf_op jit(solution)/shard_map/while/body/eval_jaxpr/all_to_all | solution.py:96
  233.7 4.8 collective-permute-start.21
  233.9 7.0 %collective-permute-start.28 = (bf16[1536,16]{0,1:T(8,128)(2,1)}, bf16[1536,16]{0,1:T(8,128)(2,1)}, u32[]{:S(2)}, u32[]{:S(2)}) collective-permute-start(bf16[1536,16]{0,1:T(8,128)(2,1)} %collective-permute-done.27), channel_id=1, source_target_pairs={{0,120},{8,0},{16,8},{24,16},{32,24},{40,32},{48,40},{56,48},{64,5... | collective-permute-start | bytes 147464 | tf_op jit(solution)/shard_map/while/body/eval_jaxpr/ppermute | solution.py:88
  238.6 5.3 collective-permute-start.22
  240.9 8.7 %collective-permute-start.29 = (bf16[1536,16]{0,1:T(8,128)(2,1)}, bf16[1536,16]{0,1:T(8,128)(2,1)S(1)}, u32[]{:S(2)}, u32[]{:S(2)}) collective-permute-start(bf16[1536,16]{0,1:T(8,128)(2,1)} %collective-permute-done.28), channel_id=1, source_target_pairs={{0,120},{8,0},{16,8},{24,16},{32,24},{40,32},{48,40},{56,48},{64,5... | collective-permute-start | bytes 147464 | tf_op jit(solution)/shard_map/while/body/eval_jaxpr/ppermute | solution.py:88
  255.3 12.0 %all-to-all-start.1 = ((bf16[96,16,16]{0,2,1:T(8,128)(2,1)}), bf16[96,16,16]{0,2,1:T(8,128)(2,1)}, u32[]{:S(2)}, u32[]{:S(2)}) async-start(bf16[96,16,16]{0,2,1:T(8,128)(2,1)} %convert_element_type.431), calls=%async_computation.1 | async-start | bytes 131072 | tf_op jit(solution)/shard_map/while/body/eval_jaxpr/all_to_all | solution.py:96
  268.3 6.0 collective-permute-start.30
  275.2 9.3 %collective-permute-start = (bf16[1536,16]{0,1:T(8,128)(2,1)S(1)}, bf16[1536,16]{0,1:T(8,128)(2,1)S(1)}, u32[]{:S(2)}, u32[]{:S(2)}) collective-permute-start(bf16[1536,16]{0,1:T(8,128)(2,1)S(1)} %bitcast_select_fusion.3), channel_id=1, source_target_pairs={{0,8},{8,16},{16,24},{24,32},{32,40},{40,48},{48,56},{56,64},{64,7... | collective-permute-start | bytes 147464 | tf_op jit(solution)/shard_map/while/body/eval_jaxpr/ppermute | solution.py:86
  275.2 14.1 %collective-permute-start.8 = (bf16[1536,16]{0,1:T(8,128)(2,1)S(1)}, bf16[1536,16]{0,1:T(8,128)(2,1)S(1)}, u32[]{:S(2)}, u32[]{:S(2)}) collective-permute-start(bf16[1536,16]{0,1:T(8,128)(2,1)S(1)} %bitcast_select_fusion.3), channel_id=1, source_target_pairs={{0,120},{8,0},{16,8},{24,16},{32,24},{40,32},{48,40},{56,48},{64,5... | collective-permute-start | bytes 147464 | tf_op jit(solution)/shard_map/while/body/eval_jaxpr/ppermute | solution.py:88
  289.2 5.3 collective-permute-start.9
  308.7 6.0 collective-permute-start.13
  312.9 4.7 collective-permute-start.7
  323.4 12.2 %all-to-all-start = ((bf16[96,16,16]{0,2,1:T(8,128)(2,1)}), bf16[96,16,16]{0,2,1:T(8,128)(2,1)S(1)}, u32[]{:S(2)}, u32[]{:S(2)}) async-start(bf16[96,16,16]{0,2,1:T(8,128)(2,1)} %convert_element_type.430), calls=%async_computation | async-start | bytes 131072 | tf_op jit(solution)/shard_map/while/body/eval_jaxpr/all_to_all | solution.py:96
  364.3 4.8 collective-permute-start.21
  364.5 7.0 %collective-permute-start.28 = (bf16[1536,16]{0,1:T(8,128)(2,1)}, bf16[1536,16]{0,1:T(8,128)(2,1)}, u32[]{:S(2)}, u32[]{:S(2)}) collective-permute-start(bf16[1536,16]{0,1:T(8,128)(2,1)} %collective-permute-done.27), channel_id=1, source_target_pairs={{0,120},{8,0},{16,8},{24,16},{32,24},{40,32},{48,40},{56,48},{64,5... | collective-permute-start | bytes 147464 | tf_op jit(solution)/shard_map/while/body/eval_jaxpr/ppermute | solution.py:88
  369.2 5.3 collective-permute-start.22
  371.5 8.7 %collective-permute-start.29 = (bf16[1536,16]{0,1:T(8,128)(2,1)}, bf16[1536,16]{0,1:T(8,128)(2,1)S(1)}, u32[]{:S(2)}, u32[]{:S(2)}) collective-permute-start(bf16[1536,16]{0,1:T(8,128)(2,1)} %collective-permute-done.28), channel_id=1, source_target_pairs={{0,120},{8,0},{16,8},{24,16},{32,24},{40,32},{48,40},{56,48},{64,5... | collective-permute-start | bytes 147464 | tf_op jit(solution)/shard_map/while/body/eval_jaxpr/ppermute | solution.py:88
  385.8 12.0 %all-to-all-start.1 = ((bf16[96,16,16]{0,2,1:T(8,128)(2,1)}), bf16[96,16,16]{0,2,1:T(8,128)(2,1)}, u32[]{:S(2)}, u32[]{:S(2)}) async-start(bf16[96,16,16]{0,2,1:T(8,128)(2,1)} %convert_element_type.431), calls=%async_computation.1 | async-start | bytes 131072 | tf_op jit(solution)/shard_map/while/body/eval_jaxpr/all_to_all | solution.py:96
  398.9 6.0 collective-permute-start.30
  405.7 9.3 %collective-permute-start = (bf16[1536,16]{0,1:T(8,128)(2,1)S(1)}, bf16[1536,16]{0,1:T(8,128)(2,1)S(1)}, u32[]{:S(2)}, u32[]{:S(2)}) collective-permute-start(bf16[1536,16]{0,1:T(8,128)(2,1)S(1)} %bitcast_select_fusion.3), channel_id=1, source_target_pairs={{0,8},{8,16},{16,24},{24,32},{32,40},{40,48},{48,56},{56,64},{64,7... | collective-permute-start | bytes 147464 | tf_op jit(solution)/shard_map/while/body/eval_jaxpr/ppermute | solution.py:86
  405.7 14.1 %collective-permute-start.8 = (bf16[1536,16]{0,1:T(8,128)(2,1)S(1)}, bf16[1536,16]{0,1:T(8,128)(2,1)S(1)}, u32[]{:S(2)}, u32[]{:S(2)}) collective-permute-start(bf16[1536,16]{0,1:T(8,128)(2,1)S(1)} %bitcast_select_fusion.3), channel_id=1, source_target_pairs={{0,120},{8,0},{16,8},{24,16},{32,24},{40,32},{48,40},{56,48},{64,5... | collective-permute-start | bytes 147464 | tf_op jit(solution)/shard_map/while/body/eval_jaxpr/ppermute | solution.py:88
  419.8 5.3 collective-permute-start.9
  439.3 6.0 collective-permute-start.13
  454.0 12.2 %all-to-all-start = ((bf16[96,16,16]{0,2,1:T(8,128)(2,1)}), bf16[96,16,16]{0,2,1:T(8,128)(2,1)S(1)}, u32[]{:S(2)}, u32[]{:S(2)}) async-start(bf16[96,16,16]{0,2,1:T(8,128)(2,1)} %convert_element_type.430), calls=%async_computation | async-start | bytes 131072 | tf_op jit(solution)/shard_map/while/body/eval_jaxpr/all_to_all | solution.py:96
  494.8 4.8 collective-permute-start.21
  495.1 7.0 %collective-permute-start.28 = (bf16[1536,16]{0,1:T(8,128)(2,1)}, bf16[1536,16]{0,1:T(8,128)(2,1)}, u32[]{:S(2)}, u32[]{:S(2)}) collective-permute-start(bf16[1536,16]{0,1:T(8,128)(2,1)} %collective-permute-done.27), channel_id=1, source_target_pairs={{0,120},{8,0},{16,8},{24,16},{32,24},{40,32},{48,40},{56,48},{64,5... | collective-permute-start | bytes 147464 | tf_op jit(solution)/shard_map/while/body/eval_jaxpr/ppermute | solution.py:88
  499.7 5.3 collective-permute-start.22
  502.1 8.7 %collective-permute-start.29 = (bf16[1536,16]{0,1:T(8,128)(2,1)}, bf16[1536,16]{0,1:T(8,128)(2,1)S(1)}, u32[]{:S(2)}, u32[]{:S(2)}) collective-permute-start(bf16[1536,16]{0,1:T(8,128)(2,1)} %collective-permute-done.28), channel_id=1, source_target_pairs={{0,120},{8,0},{16,8},{24,16},{32,24},{40,32},{48,40},{56,48},{64,5... | collective-permute-start | bytes 147464 | tf_op jit(solution)/shard_map/while/body/eval_jaxpr/ppermute | solution.py:88
  516.4 12.0 %all-to-all-start.1 = ((bf16[96,16,16]{0,2,1:T(8,128)(2,1)}), bf16[96,16,16]{0,2,1:T(8,128)(2,1)}, u32[]{:S(2)}, u32[]{:S(2)}) async-start(bf16[96,16,16]{0,2,1:T(8,128)(2,1)} %convert_element_type.431), calls=%async_computation.1 | async-start | bytes 131072 | tf_op jit(solution)/shard_map/while/body/eval_jaxpr/all_to_all | solution.py:96
  529.4 6.0 collective-permute-start.30
  (303 other events, 2914.1 us)
Sparse Core Ops, SparseCore 0:
  536.7 84.9 all-reduce.21
